TPU v7x, 1024 devices: a whole 8x8x8 slice. The times are simulated.
1024 devices in a mesh: dp: 8 (over z_lo, core), hidden: 16 (over x, z_hi), mp: 8 (over y).
Axes of the slice: x: 8, y: 8, z: 8 (z_hi: 2, z_lo: 4; z = z_hi * 4 + z_lo), core: 2. Of those that a mesh axis runs over, the one named last changes fastest.
Arguments:
- activations: bfloat16 [4096, 26624], P('dp', 'hidden'), may hold values from -6 to 6
- weight: bfloat16 [26624, 8192], P('hidden', 'mp'), may hold values from -0.0390625 to 0.0390625
- out_grad: bfloat16 [4096, 8192], P(('dp', 'hidden'), 'mp'), may hold values from -0.25 to 0.25
- momentum: float32 [8, 3328, 8192], P('dp', 'hidden', 'mp'), may hold values from -6 to 6
Outputs:
- output: bfloat16 [4096, 8192], P(('dp', 'hidden'), 'mp')
- new_momentum: float32 [8, 3328, 8192], P('dp', 'hidden', 'mp')
- new_weight: bfloat16 [8, 3328, 8192], P('dp', 'hidden', 'mp')
All inputs are finite; a program needn't handle non-finite values.
Results may differ from a plain program's by a relative error of at most 0.015.
Values may be sent and summed in bfloat16 or wider, within the bound.
No kernel may reach another device: no remote copies, remote signals or barrier semaphores. Data moves between devices by JAX's collectives and lax.ppermute only.
A program may use at most 32 MiB of HBM per device.

v0:
```python
import jax
import jax.numpy as jnp
from jax import lax
from jax.sharding import PartitionSpec as P

momentum_decay = 0.9
step_size = 0.05


def on_device(activations, weight, out_grad, momentum):
    slab_rows = momentum.shape[1]
    act_rows = activations
    summed = lax.psum_scatter(
        jnp.dot(act_rows, weight, preferred_element_type=jnp.float32).astype(jnp.bfloat16),
        "hidden",
        scatter_dimension=0,
        tiled=True,
    )
    act_rows = activations
    local_grad = lax.dot_general(
        act_rows,
        lax.all_gather(out_grad, "hidden", axis=0, tiled=True),
        (((0,), (0,)), ((), ())),
        preferred_element_type=jnp.float32,
    )
    grad_share = lax.psum_scatter(
        local_grad.astype(jnp.bfloat16), "dp", scatter_dimension=0, tiled=True
    ).astype(jnp.float32)
    new_momentum = momentum_decay * momentum + grad_share[None]
    own_rows = lax.dynamic_slice_in_dim(weight, lax.axis_index("dp") * slab_rows, slab_rows, 0)
    new_weight = (own_rows.astype(jnp.float32)[None] - step_size * new_momentum).astype(
        jnp.bfloat16
    )
    return (summed, new_momentum, new_weight)


def solution(mesh):
    placed = (
        P("dp", "hidden"),
        P("hidden", "mp"),
        P(("dp", "hidden"), "mp"),
        P("dp", "hidden", "mp"),
    )
    return jax.shard_map(
        on_device,
        mesh=mesh,
        in_specs=placed,
        out_specs=(P(("dp", "hidden"), "mp"), P("dp", "hidden", "mp"), P("dp", "hidden", "mp")),
        check_vma=False,
    )
```

profile of v0, /device:TPU:4, one launch (start us, length us, event | category | flops | bytes accessed | tf_op | source)
XLA Modules:
  0.0 417.6 jit_solution(10519053062874067654)
XLA Ops:
  7.2 0.0 copy-start
  7.2 0.0 all-gather.2.cloned.1.call-start
  7.2 0.7 all-gather.2.cloned.1.call-update
  7.9 0.0 reduce-scatter.5.cloned.1.call-start
  8.0 114.7 %all-gather.2.cloned.1.call-done = bf16[512,1024]{1,0:T(8,128)(2,1)} async-done(((bf16[32,1024]{1,0:T(8,128)(2,1)}), bf16[512,1024]{1,0:T(8,128)(2,1)}) %all-gather.2.cloned.1.call-update) | async-done | bytes 1048592 | tf_op jit(solution)/shard_map/all_gather | solution.py:22
  122.6 0.0 copy-done
  122.6 4.9 %convolution_convert_fusion = bf16[1664,1024]{1,0:T(8,128)(2,1)} fusion(bf16[512,1664]{1,0:T(8,128)(2,1)S(1)} %copy-done, bf16[512,1024]{1,0:T(8,128)(2,1)} %all-gather.2.cloned.1.call-done), kind=kOutput, calls=%fused_computation | convolution fusion | flops 1746534400 | bytes 6160384 | tf_op jit(solution)/shard_map/dot_general | solution.py:20
  127.6 0.0 reduce-scatter.5.cloned.1.call-update
  127.6 0.0 copy-start.1
  127.6 0.0 reduce-scatter.3.cloned.1.call-start
  127.6 5.1 %convolution_convert_fusion.1 = bf16[512,1024]{1,0:T(8,128)(2,1)} fusion(bf16[512,1664]{1,0:T(8,128)(2,1)S(1)} %copy-done, bf16[1664,1024]{1,0:T(8,128)(2,1)} %param.5), kind=kOutput, calls=%fused_computation.1 | convolution fusion | flops 1745354752 | bytes 6160384 | tf_op jit(solution)/shard_map/dot_general | solution.py:14
  132.7 0.0 reduce-scatter.3.cloned.1.call-update
  132.7 43.1 %reduce-scatter.5.cloned.1.call-done = bf16[208,1024]{1,0:T(8,128)(2,1)} async-done(((bf16[1664,1024]{1,0:T(8,128)(2,1)}), bf16[208,1024]{1,0:T(8,128)(2,1)}) %reduce-scatter.5.cloned.1.call-update) | async-done | bytes 426000 | tf_op jit(solution)/shard_map/reduce_scatter | solution.py:26
  175.9 0.0 copy-done.1
  175.9 2.4 fusion
  178.3 232.8 %reduce-scatter.3.cloned.1.call-done = bf16[32,1024]{1,0:T(8,128)(2,1)} async-done(((bf16[512,1024]{1,0:T(8,128)(2,1)}), bf16[32,1024]{1,0:T(8,128)(2,1)}) %reduce-scatter.3.cloned.1.call-update) | async-done | bytes 65552 | tf_op jit(solution)/shard_map/reduce_scatter | solution.py:13
Async XLA Ops:
  7.2 115.5 %copy-start = (bf16[512,1664]{1,0:T(8,128)(2,1)S(1)}, bf16[512,1664]{1,0:T(8,128)(2,1)}, u32[]{:S(2)}) copy-start(bf16[512,1664]{1,0:T(8,128)(2,1)} %param.4) | copy-start | bytes 5111812
  7.2 115.5 %all-gather.2.cloned.1.call-start = ((), (), s32[]{:S(2)}) async-start(), calls=%async_computation.3 | async-start | bytes 1114112 | tf_op jit(solution)/shard_map/all_gather | solution.py:22
  7.9 168.0 %reduce-scatter.5.cloned.1.call-start = ((), (), s32[]{:S(2)}) async-start(), calls=%async_computation.4 | async-start | bytes 3833856 | tf_op jit(solution)/shard_map/reduce_scatter | solution.py:26
  127.6 48.3 %copy-start.1 = (f32[1,208,1024]{2,1,0:T(8,128)S(1)}, f32[1,208,1024]{2,1,0:T(8,128)}, u32[]{:S(2)}) copy-start(f32[1,208,1024]{2,1,0:T(8,128)} %param.7) | copy-start | bytes 2555908
  127.6 283.5 %reduce-scatter.3.cloned.1.call-start = ((), (), s32[]{:S(2)}) async-start(), calls=%async_computation.2 | async-start | bytes 1114112 | tf_op jit(solution)/shard_map/reduce_scatter | solution.py:13
Sparse Core Ops, SparseCore 0:
  12.4 110.2 all-gather.1
  127.7 48.1 reduce-scatter.4
  182.1 228.9 reduce-scatter.2
where the time goes:
time: 418 us
  waiting for transfers between devices  391 us (94%)
  between operations  13.8 us (3%)
  matrix products  9.98 us (2%)
    reduce_scatter x1, waiting for transfers between devices, on_device(): lax.psum_scatter(jnp.dot(act_rows, weight, preferred_element_type=jnp.flo...  233 us
    all_gather x1, waiting for transfers between devices, on_device(): lax.all_gather(out_grad, 'hidden', axis=0, tiled=True)  115 us
    reduce_scatter x1, waiting for transfers between devices, on_device(): lax.psum_scatter(local_grad.astype(jnp.bfloat16), 'dp', scatter_dimension...  43.1 us
  transfers between devices with their start and end apart: 3, of which 3 were waited for; matrix products, arithmetic and copies ran while one was open for 2% of the time, Pallas kernels for 0%

commit v1 on v0

--- a/solution.py
+++ b/solution.py
@@ -9,23 +9,34 @@
 
 def on_device(activations, weight, out_grad, momentum):
     slab_rows = momentum.shape[1]
-    act_rows = activations
-    summed = lax.psum_scatter(
-        jnp.dot(act_rows, weight, preferred_element_type=jnp.float32).astype(jnp.bfloat16),
+    tokens = activations.shape[0]
+    own_tokens, cols = out_grad.shape
+    blocks = tokens // own_tokens
+    gathered = lax.all_to_all(
+        jnp.broadcast_to(out_grad[None], (blocks, own_tokens, cols)),
         "hidden",
-        scatter_dimension=0,
+        split_axis=0,
+        concat_axis=0,
         tiled=True,
-    )
-    act_rows = activations
+    ).reshape(tokens, cols)
     local_grad = lax.dot_general(
-        act_rows,
-        lax.all_gather(out_grad, "hidden", axis=0, tiled=True),
+        activations,
+        gathered,
         (((0,), (0,)), ((), ())),
         preferred_element_type=jnp.float32,
     )
     grad_share = lax.psum_scatter(
         local_grad.astype(jnp.bfloat16), "dp", scatter_dimension=0, tiled=True
     ).astype(jnp.float32)
+    partial_out = jnp.dot(activations, weight, preferred_element_type=jnp.float32)
+    pieces = lax.all_to_all(
+        partial_out.astype(jnp.bfloat16).reshape(blocks, own_tokens, cols),
+        "hidden",
+        split_axis=0,
+        concat_axis=0,
+        tiled=True,
+    )
+    summed = jnp.sum(pieces.astype(jnp.float32), axis=0).astype(jnp.bfloat16)
     new_momentum = momentum_decay * momentum + grad_share[None]
     own_rows = lax.dynamic_slice_in_dim(weight, lax.axis_index("dp") * slab_rows, slab_rows, 0)
     new_weight = (own_rows.astype(jnp.float32)[None] - step_size * new_momentum).astype(

time: 418 us -> 149 us (0.36)
  the two profiles are of different devices: /device:TPU:4 before, /device:TPU:8 now
where the time goes in v1:
time: 149 us
  waiting for transfers between devices  63.7 us (43%)
  blocking collectives  50.1 us (34%)
  between operations  14 us (9%)
  matrix products  8.75 us (6%)
  starting transfers between devices  7.88 us (5%)
  other arithmetic  3.5 us (2%)
    all_to_all x1, blocking collectives, on_device(): lax.all_to_all(jnp.broadcast_to(out_grad[None], (blocks, own_tokens, cols...  50.1 us
    all_to_all x1, waiting for transfers between devices, on_device(): lax.all_to_all(partial_out.astype(jnp.bfloat16).reshape(blocks, own_token...  38.8 us
    reduce_scatter x1, waiting for transfers between devices, on_device(): lax.psum_scatter(local_grad.astype(jnp.bfloat16), 'dp', scatter_dimension...  24.9 us
    all_to_all x1, starting transfers between devices, on_device(): lax.all_to_all(partial_out.astype(jnp.bfloat16).reshape(blocks, own_token...  7.84 us
    dot_general x1, matrix products, on_device(): jnp.dot(activations, weight, preferred_element_type=jnp.float32)  5.04 us
    dot_general x1, matrix products, on_device(): lax.dot_general(activations, gathered, (((0,), (0,)), ((), ())), preferre...  3.72 us
  transfers between devices with their start and end apart: 2, of which 2 were waited for; matrix products, arithmetic and copies ran while one was open for 4% of the time, Pallas kernels for 0%

profile of v1, /device:TPU:8, one launch (start us, length us, event | category | flops | bytes accessed | tf_op | source)
XLA Modules:
  0.0 149.0 jit_solution(6012011348651313434)
XLA Ops:
  7.2 0.0 copy-start
  7.2 0.0 reduce-scatter.2.cloned.1.call-start
  7.2 1.1 broadcast_in_dim.18
  8.3 50.1 %all_to_all.10 = bf16[16,32,1024]{2,1,0:T(8,128)(2,1)S(1)} all-to-all(bf16[16,32,1024]{2,1,0:T(8,128)(2,1)S(1)} %broadcast_in_dim.18), channel_id=1, replica_groups=mesh['dp'=8,'hidden'=16,'mp'=8] {'hidden'}, dimensions={0} | all-to-all | bytes 2097152 | tf_op jit(solution)/shard_map/all_to_all | solution.py:15
  58.4 0.0 copy-done
  58.4 3.7 %convolution_convert_fusion = bf16[1664,1024]{1,0:T(8,128)(2,1)} fusion(bf16[512,1664]{1,0:T(8,128)(2,1)S(1)} %copy-done, bf16[512,1024]{1,0:T(8,128)(2,1)S(1)} %bitcast.14), kind=kOutput, calls=%fused_computation | convolution fusion | flops 1746534400 | bytes 6160384 | tf_op jit(solution)/shard_map/dot_general | solution.py:22
  62.1 0.0 reduce-scatter.2.cloned.1.call-update
  62.1 5.0 %convolution_convert_fusion.1 = bf16[512,1024]{1,0:T(8,128)(2,1)} fusion(bf16[512,1664]{1,0:T(8,128)(2,1)S(1)} %copy-done, bf16[1664,1024]{1,0:T(8,128)(2,1)} %param.5), kind=kOutput, calls=%fused_computation.1 | convolution fusion | flops 1745354752 | bytes 6160384 | tf_op jit(solution)/shard_map/dot_general | solution.py:31
  67.2 7.8 %all-to-all-start = ((bf16[16,32,1024]{2,1,0:T(8,128)(2,1)}), bf16[16,32,1024]{2,1,0:T(8,128)(2,1)S(1)}, u32[]{:S(2)}, u32[]{:S(2)}) async-start(bf16[16,32,1024]{2,1,0:T(8,128)(2,1)} %bitcast.13), calls=%async_computation | async-start | bytes 2097152 | tf_op jit(solution)/shard_map/all_to_all | solution.py:32
  75.0 38.8 %all-to-all-done = bf16[16,32,1024]{2,1,0:T(8,128)(2,1)S(1)} async-done(((bf16[16,32,1024]{2,1,0:T(8,128)(2,1)}), bf16[16,32,1024]{2,1,0:T(8,128)(2,1)S(1)}, u32[]{:S(2)}, u32[]{:S(2)}) %all-to-all-start) | async-done | bytes 1048608 | tf_op jit(solution)/shard_map/all_to_all | solution.py:32
  113.8 0.8 reduce_sum.12
  114.6 24.9 %reduce-scatter.2.cloned.1.call-done = bf16[208,1024]{1,0:T(8,128)(2,1)} async-done(((bf16[1664,1024]{1,0:T(8,128)(2,1)}), bf16[208,1024]{1,0:T(8,128)(2,1)}) %reduce-scatter.2.cloned.1.call-update) | async-done | bytes 426000 | tf_op jit(solution)/shard_map/reduce_scatter | solution.py:28
  139.5 2.7 %fusion = (bf16[1,208,1024]{2,1,0:T(8,128)(2,1)}, f32[1,208,1024]{2,1,0:T(8,128)}) fusion(bf16[1664,1024]{1,0:T(8,128)(2,1)} %param.5, s32[]{:T(128)S(6)} %select_n.3, bf16[208,1024]{1,0:T(8,128)(2,1)} %reduce-scatter.2.cloned.1.call-done, f32[1,208,1024]{2,1,0:T(8,128)} %param.7), kind=kLoop, calls=%fused_computation.3 | loop fusion | flops 1490944 | bytes 2981892 | tf_op jit(solution)/shard_map/convert_element_type | solution.py:42
Async XLA Ops:
  7.2 51.2 %copy-start = (bf16[512,1664]{1,0:T(8,128)(2,1)S(1)}, bf16[512,1664]{1,0:T(8,128)(2,1)}, u32[]{:S(2)}) copy-start(bf16[512,1664]{1,0:T(8,128)(2,1)} %param.4) | copy-start | bytes 5111812
  7.2 132.3 %reduce-scatter.2.cloned.1.call-start = ((), (), s32[]{:S(2)}) async-start(), calls=%async_computation.3 | async-start | bytes 3833856 | tf_op jit(solution)/shard_map/reduce_scatter | solution.py:28
  67.2 46.6 %all-to-all-start = ((bf16[16,32,1024]{2,1,0:T(8,128)(2,1)}), bf16[16,32,1024]{2,1,0:T(8,128)(2,1)S(1)}, u32[]{:S(2)}, u32[]{:S(2)}) async-start(bf16[16,32,1024]{2,1,0:T(8,128)(2,1)} %bitcast.13), calls=%async_computation | async-start | bytes 2097152 | tf_op jit(solution)/shard_map/all_to_all | solution.py:32
Sparse Core Ops, SparseCore 0:
  62.3 77.1 reduce-scatter.1
